TPU v7x, 32 devices: a whole 2x2x4 slice. The times are simulated.
32 devices in a mesh: member: 2 (over x), wave: 16 (over z, y, core).
Axes of the slice: x: 2, y: 2, z: 4, core: 2. Of those that a mesh axis runs over, the one named last changes fastest.
Arguments:
- spectral: bfloat16 [1024, 2, 256, 192], P(('member', 'wave')), parts along dimension 0, may hold values from -6 to 6
- basis: bfloat16 [512, 2, 256, 256], P('wave'), may hold values from -0.25 to 0.25
- quad_weights: float32 [256], replicated, may hold values from 0.5 to 2
- column: float32 [96, 96], replicated, may hold values from -0.625 to 0.625
- square_coef: float32 [96], replicated, may hold values from -0.3 to 0.3
- cube_coef: float32 [96], replicated, may hold values from 0.05 to 0.2
- trunc: int32 [256], replicated, may hold values from 16 to 512, as said below
Outputs:
- new_spectral: bfloat16 [1024, 2, 256, 192], P(('member', 'wave')), parts along dimension 0
There are 2 independent parts, one for each index of `member`. A program takes and returns all parts, laid end to end along the dimension named above; an argument that names none is the same for every part. Nothing has to cross between parts.
Inputs may be any that keep to these rules, and one draw needn't show every extreme that they name: `trunc`: rows nearer the equator never keep fewer wavenumbers than rows nearer the pole.
All inputs are finite; a program needn't handle non-finite values.
Results may differ from a plain program's by a relative error of at most 0.0057.
Values may be sent and summed in bfloat16 or wider, within the bound.
No kernel may reach another device: no remote copies, remote signals or barrier semaphores. Data moves between devices by JAX's collectives and lax.ppermute only.
A program may use at most 128 MiB of HBM per device.

v0:
```python
import math
import jax
import jax.numpy as jnp
from jax import lax
from jax.sharding import PartitionSpec as P

NLON = 1024


def fourier_table(wave_count, lon_count):
    wave_ids = jnp.arange(wave_count, dtype=jnp.int32)
    lon_ids = jnp.arange(lon_count, dtype=jnp.int32)
    phases = wave_ids[:, None] * lon_ids[None, :] % NLON
    angles = phases.astype(jnp.float32) * (2.0 * math.pi / NLON)
    return jnp.stack([jnp.cos(angles), -jnp.sin(angles)], axis=1).astype(jnp.bfloat16)


def per_device(spectral, basis, quad_weights, column, square_coef, cube_coef, trunc):
    devices = lax.axis_size("wave")
    position = lax.axis_index("wave")
    local_waves = spectral.shape[0]
    half_slots = spectral.shape[2]
    channels = spectral.shape[3]
    levels = channels // 2
    half_lats = basis.shape[3]
    wave_ids = position * local_waves + jnp.arange(local_waves, dtype=jnp.int32)
    degrees = (
        wave_ids[:, None, None]
        + 2 * jnp.arange(half_slots, dtype=jnp.int32)[None, None, :]
        + jnp.arange(2, dtype=jnp.int32)[None, :, None]
    )
    in_range = (degrees < 2 * half_slots)[..., None]
    spec_in = jnp.where(in_range, spectral, jnp.zeros_like(spectral))
    parities = jnp.einsum("mpkj,mpkc->mpjc", basis, spec_in, preferred_element_type=jnp.float32)
    north_rows = parities[:, 0] + parities[:, 1]
    south_rows = parities[:, 0] - parities[:, 1]
    pair_rows = half_lats // devices
    pair_lats = position * pair_rows + jnp.arange(pair_rows, dtype=jnp.int32)
    packed = jnp.stack([north_rows, south_rows], axis=1).astype(jnp.bfloat16)
    arrived = lax.all_to_all(packed, "wave", split_axis=2, concat_axis=0, tiled=True)
    coeffs = arrived.reshape(arrived.shape[0], 2 * pair_rows, channels)
    row_lats = jnp.concatenate([pair_lats, pair_lats])
    total_waves = coeffs.shape[0]
    grid_rows = coeffs.shape[1]
    trunc_rows = trunc[row_lats]
    weight_rows = quad_weights[row_lats]
    kept_mask = (jnp.arange(total_waves, dtype=jnp.int32)[:, None] < trunc_rows[None, :])[..., None]
    coeffs = jnp.where(kept_mask, coeffs, jnp.zeros_like(coeffs))
    coeff_four = coeffs.reshape(total_waves, grid_rows, 2, levels)
    fourier = fourier_table(total_waves, NLON)
    grid_temp = jnp.einsum("mgrv,mrx->gvx", coeff_four, fourier, preferred_element_type=jnp.float32)
    grid_temp = grid_temp * (1.0 / math.sqrt(total_waves))
    column_mix = jnp.einsum("uv,gvx->gux", column, grid_temp, precision=lax.Precision.HIGHEST)
    tendency = (
        column_mix
        + square_coef[None, :, None] * grid_temp * grid_temp
        - cube_coef[None, :, None] * grid_temp * grid_temp * grid_temp
    )
    partial_sum = jnp.sum(tendency * weight_rows[:, None, None], axis=(0, 2))
    level_total = lax.psum(partial_sum, "wave")
    level_mean = level_total / (NLON * 2.0 * jnp.sum(quad_weights))
    shifted = (tendency - level_mean[None, :, None]).astype(jnp.bfloat16)
    analysed = jnp.einsum(
        "gvx,mrx->mgrv", shifted, fourier, preferred_element_type=jnp.float32
    ) * math.sqrt(2.0 / NLON)
    analysed = analysed.reshape(total_waves, grid_rows, channels)
    analysed = jnp.where(kept_mask, analysed, 0.0).astype(jnp.bfloat16)
    settled = lax.optimization_barrier(analysed).astype(jnp.float32)
    north_back = settled[:, :pair_rows]
    south_back = settled[:, pair_rows:]
    weight = quad_weights[pair_lats][None, :, None]
    folded_part = jnp.stack(
        [weight * (north_back + south_back), weight * (north_back - south_back)], axis=1
    ).astype(jnp.bfloat16)
    folded = lax.all_to_all(folded_part, "wave", split_axis=0, concat_axis=2, tiled=True)
    direct = jnp.einsum("mpkj,mpjc->mpkc", basis, folded, preferred_element_type=jnp.float32)
    return jnp.where(in_range, spec_in.astype(jnp.float32) + direct, 0.0).astype(jnp.bfloat16)


def solution(mesh):
    return jax.shard_map(
        per_device,
        mesh=mesh,
        in_specs=(
            P(("member", "wave"), None, None, None),
            P("wave", None, None, None),
            P(),
            P(),
            P(),
            P(),
            P(),
        ),
        out_specs=P(("member", "wave"), None, None, None),
        check_vma=False,
    )
```

profile of v0, /device:TPU:1, one launch (start us, length us, event | category | flops | bytes accessed | tf_op | source)
XLA Modules:
  0.0 613.8 jit_solution(11071485273975315123)
XLA Ops:
  0.0 0.0 copy-start
  0.0 0.1 broadcast_add_fusion
  0.1 7.0 %fusion.14 = f32[32,2,256,192]{2,3,1,0:T(8,128)S(1)} fusion(bf16[32,2,256,256]{3,2,1,0:T(8,128)(2,1)} %param.8, bf16[32,2,256,192]{2,3,1,0:T(8,128)(2,1)} %param.7, pred[32,2,256]{2,1,0:T(4,128)(4,1)S(1)} %add_compare_fusion), kind=kOutput, calls=%fused_computation.34 | convolution fusion | flops 1613758464 | bytes 27279360 | tf_op jit(solution)/shard_map/mpkj,mpkc->mpjc/dot_general | solution.py:34
  7.2 2.7 add_convert_fusion
  9.8 5.2 pad_maximum_fusion
  15.0 21.1 %copy.19 = bf16[32,2,256,192]{3,1,0,2:T(2,128)(2,1)} copy(bf16[32,2,256,192]{2,3,1,0:T(8,128)(2,1)} %pad_maximum_fusion) | data formatting | bytes 12582912 | tf_op jit(solution)/shard_map/stack | solution.py:39
  36.1 7.9 %all-to-all-start = ((bf16[32,2,256,192]{3,1,0,2:T(2,128)(2,1)}), bf16[32,2,256,192]{3,1,0,2:T(2,128)(2,1)}, u32[]{:S(2)}, u32[]{:S(2)}) async-start(bf16[32,2,256,192]{3,1,0,2:T(2,128)(2,1)} %copy.19), calls=%async_computation | async-start | bytes 16777216 | tf_op jit(solution)/shard_map/all_to_all | solution.py:40
  44.1 0.6 reduce_sum.19
  44.7 0.1 fusion.30
  44.8 0.7 gather_fusion.2
  45.5 0.7 gather_fusion.1
  46.2 0.7 gather_fusion
  46.9 0.1 copy.18
  47.7 8.5 %negate_convert_fusion = (bf16[512,1,1024]{2,0,1:T(8,128)(2,1)S(1)}, bf16[512,1,1024]{2,0,1:T(8,128)(2,1)S(1)}) fusion(), kind=kLoop, calls=%fused_computation.47 | loop fusion | flops 8912896 | bytes 2097152 | tf_op jit(solution)/shard_map/convert.7
  56.2 138.8 %all-to-all-done = bf16[32,2,256,192]{3,1,0,2:T(2,128)(2,1)} async-done(((bf16[32,2,256,192]{3,1,0,2:T(2,128)(2,1)}), bf16[32,2,256,192]{3,1,0,2:T(2,128)(2,1)}, u32[]{:S(2)}, u32[]{:S(2)}) %all-to-all-start) | async-done | bytes 6291488 | tf_op jit(solution)/shard_map/all_to_all | solution.py:40
  195.1 13.4 %copy.20 = bf16[32,2,256,192]{3,2,1,0:T(8,128)(2,1)} copy(bf16[32,2,256,192]{3,1,0,2:T(2,128)(2,1)} %all-to-all-done) | data formatting | bytes 12582912 | tf_op jit(solution)/shard_map/all_to_all | solution.py:40
  208.5 7.9 %copy.21 = bf16[16,32,2,16,192]{4,3,2,1,0:T(8,128)(2,1)} copy(bf16[16,32,2,16,192]{4,3,0,2,1:T(8,128)(2,1)} %bitcast.75) | data formatting | bytes 12582912 | tf_op jit(solution)/shard_map/all_to_all | solution.py:40
  216.4 13.8 %reshape.210 = bf16[512,32,2,96]{3,2,1,0:T(2,128)(2,1)} reshape(bf16[16,32,2,16,192]{4,3,2,1,0:T(8,128)(2,1)} %copy.21) | data formatting | bytes 12582912 | tf_op jit(solution)/shard_map/reshape | solution.py:41
  230.2 23.7 %broadcast_select_fusion = bf16[512,32,2,96]{3,2,1,0:T(2,128)(2,1)S(1)} fusion(bf16[512,32,2,96]{3,2,1,0:T(2,128)(2,1)} %reshape.210, pred[512,32]{1,0:T(8,128)(4,1)S(1)} %iota_compare_fusion), kind=kLoop, calls=%fused_computation.4 | loop fusion | flops 3145728 | bytes 12599296 | tf_op jit(solution)/shard_map/jit(_where)/select_n | solution.py:48
  253.9 26.1 %fusion.6 = f32[32,96,1024,1]{2,1,3,0:T(8,128)} fusion(bf16[512,32,2,96]{3,2,1,0:T(2,128)(2,1)S(1)} %broadcast_select_fusion, bf16[512,1,1024]{2,0,1:T(8,128)(2,1)S(1)} %get-tuple-element.11, bf16[512,1,1024]{2,0,1:T(8,128)(2,1)S(1)} %get-tuple-element.12), kind=kOutput, calls=%fused_computation.20 | convolution fusion | flops 6443499520 | bytes 20971520 | tf_op jit(solution)/shard_map/mgrv,mrx->gvx/dot_general | solution.py:51
  280.0 25.0 %multiply_reduce_fusion = (f32[96]{0:T(128)S(1)}, f32[32,96,1024]{2,1,0:T(8,128)}) fusion(f32[32]{0:T(128)S(1)} %gather_fusion.2, f32[96]{0:T(128)S(1)} %get-tuple-element.13, f32[96]{0:T(128)S(1)} %get-tuple-element.14, f32[32,96,1024,1]{2,1,3,0:T(8,128)} %fusion.6, f32[96,96]{1,0:T(8,128)S(1)} %copy-done), kind=kOutput, calls=%fused_computation.19 | convolution fusion | flops 3658481664 | bytes 25203968 | tf_op jit(solution)/shard_map/uv,gvx->gux/dot_general | solution.py:53
  305.1 59.4 %psum.7 = f32[96]{0:T(128)S(1)} all-reduce(f32[96]{0:T(128)S(1)} %get-tuple-element.9), channel_id=1, replica_groups=mesh['member'=2,'wave'=16] {'wave'}, use_global_device_ids=true, to_apply=%region_1.2 | all-reduce | flops 96 | bytes 768 | tf_op jit(solution)/shard_map/psum | solution.py:60
  364.5 12.2 %multiply_bitcast_fusion = bf16[512,32,2,96]{0,3,1,2:T(8,128)(2,1)S(1)} fusion(f32[32,96,1024]{2,1,0:T(8,128)} %get-tuple-element.10, f32[96]{0:T(128)S(1)} %broadcast_divide_fusion, bf16[512,1,1024]{2,0,1:T(8,128)(2,1)S(1)} %get-tuple-element.11, bf16[512,1,1024]{2,0,1:T(8,128)(2,1)S(1)} %get-tuple-element.12), kind=kOutput, calls=%fused_computation.17 | convolution fusion | flops 6459228160 | bytes 20971904 | tf_op jit(solution)/shard_map/gvx,mrx->mgrv/dot_general | solution.py:63
  376.7 0.7 copy.23
  377.4 2.2 fusion.3
  379.6 1.7 convert_element_type.38
  381.3 2.7 fusion.17
  384.0 3.2 pad_maximum_fusion.1
  387.2 14.2 %copy.24 = bf16[512,2,16,192]{3,2,1,0:T(8,128)(2,1)} copy(bf16[512,2,16,192]{0,3,2,1:T(8,128)(2,1)} %pad_maximum_fusion.1) | data formatting | bytes 12582912 | tf_op jit(solution)/shard_map/stack | solution.py:72
  401.4 192.1 %all_to_all.33 = bf16[512,2,16,192]{3,2,1,0:T(8,128)(2,1)} all-to-all(bf16[512,2,16,192]{3,2,1,0:T(8,128)(2,1)} %copy.24), channel_id=1, replica_groups=mesh['member'=2,'wave'=16] {'wave'}, dimensions={0} | all-to-all | bytes 12582912 | tf_op jit(solution)/shard_map/all_to_all | solution.py:75
  593.5 7.8 %copy.25 = bf16[32,2,16,16,192]{4,3,2,1,0:T(8,128)(2,1)} copy(bf16[32,2,16,16,192]{4,3,1,0,2:T(8,128)(2,1)} %bitcast.76) | data formatting | bytes 12582912 | tf_op jit(solution)/shard_map/all_to_all | solution.py:75
  601.3 12.3 %fusion.2 = bf16[32,2,256,192]{2,3,1,0:T(8,128)(2,1)} fusion(pred[32,2,256]{2,1,0:T(4,128)(4,1)S(1)} %add_compare_fusion, bf16[32,2,256,192]{2,3,1,0:T(8,128)(2,1)} %param.7, bf16[32,2,256,192]{3,2,1,0:T(8,128)(2,1)} %bitcast.77, bf16[32,2,256,256]{3,2,1,0:T(8,128)(2,1)} %param.8), kind=kOutput, calls=%fused_computation.8 | convolution fusion | flops 1626341376 | bytes 27279360 | tf_op jit(solution)/shard_map/mpkj,mpjc->mpkc/dot_general | solution.py:76
  (21 shorter events, 0.2 us)
Async XLA Ops:
  0.0 280.0 %copy-start = (f32[96,96]{1,0:T(8,128)S(1)}, f32[96,96]{1,0:T(8,128)}, u32[]{:S(2)}) copy-start(f32[96,96]{1,0:T(8,128)} %param.10) | copy-start | bytes 110596
  36.1 8.0 %copy-start.2 = (f32[256]{0:T(256)S(1)}, f32[256]{0:T(256)}, u32[]{:S(2)}) copy-start(f32[256]{0:T(256)} %param.9) | copy-start | bytes 3076
  36.1 9.4 %copy-start.3 = (s32[256]{0:T(256)S(1)}, s32[256]{0:T(256)}, u32[]{:S(2)}) copy-start(s32[256]{0:T(256)} %param.13) | copy-start | bytes 3076
  36.1 11.6 %copy-start.4 = (f32[96]{0:T(128)S(1)}, f32[96]{0:T(128)}, u32[]{:S(2)}) copy-start(f32[96]{0:T(128)} %param.12) | copy-start | bytes 1156
  36.1 11.6 %copy-start.5 = (f32[96]{0:T(128)S(1)}, f32[96]{0:T(128)}, u32[]{:S(2)}) copy-start(f32[96]{0:T(128)} %param.11) | copy-start | bytes 1156
  36.1 158.9 %all-to-all-start = ((bf16[32,2,256,192]{3,1,0,2:T(2,128)(2,1)}), bf16[32,2,256,192]{3,1,0,2:T(2,128)(2,1)}, u32[]{:S(2)}, u32[]{:S(2)}) async-start(bf16[32,2,256,192]{3,1,0,2:T(2,128)(2,1)} %copy.19), calls=%async_computation | async-start | bytes 16777216 | tf_op jit(solution)/shard_map/all_to_all | solution.py:40
  601.3 12.3 %copy-start.1 = (f32[96,96]{1,0:T(8,128)S(1)}, f32[96,96]{1,0:T(8,128)}, u32[]{:S(2)}) copy-start(f32[96,96]{1,0:T(8,128)} %param.10) | copy-start | bytes 110596
where the time goes:
time: 619 us; the launch traced here: 614 us
  blocking collectives  251 us (41%)
  waiting for transfers between devices  139 us (22%)
  matrix products  82.6 us (13%)
  local copies, waits for them, and re-layouts  81.2 us (13%)
  other arithmetic  50.7 us (8%)
  starting transfers between devices  7.92 us (1%)
    all_to_all x1, blocking collectives, per_device(): lax.all_to_all(folded_part, 'wave', split_axis=0, concat_axis=2, tiled=True)  192 us
    all_to_all x1, waiting for transfers between devices, per_device(): lax.all_to_all(packed, 'wave', split_axis=2, concat_axis=0, tiled=True)  139 us
    psum x1, blocking collectives, per_device(): level_total = lax.psum(partial_sum, 'wave')  59.4 us
    dot_general x1, matrix products, per_device(): jnp.einsum('mgrv,mrx->gvx', coeff_four, fourier, preferred_element_type=j...  26.1 us
    dot_general x1, matrix products, per_device(): jnp.einsum('uv,gvx->gux', column, grid_temp, precision=lax.Precision.HIGH...  25 us
    select_n x1, other arithmetic, per_device(): coeffs = jnp.where(kept_mask, coeffs, jnp.zeros_like(coeffs))  23.7 us
    all_to_all x2, local copies, waits for them, and re-layouts, per_device(): lax.all_to_all(packed, 'wave', split_axis=2, concat_axis=0, tiled=True)  21.4 us
    another operation x1, local copies, waits for them, and re-layouts, per_device(): packed = jnp.stack([north_rows, south_rows], axis=1).astype(jnp.bfloat16)  21.1 us
  transfers between devices with their start and end apart: 1, of which 1 were waited for; matrix products, arithmetic and copies ran while one was open for 2% of the time, Pallas kernels for 0%

commit v1 on v0

--- a/solution.py
+++ b/solution.py
@@ -57,7 +57,11 @@
         - cube_coef[None, :, None] * grid_temp * grid_temp * grid_temp
     )
     partial_sum = jnp.sum(tendency * weight_rows[:, None, None], axis=(0, 2))
-    level_total = lax.psum(partial_sum, "wave")
+    level_total = partial_sum
+    for hop in (1, 2, 4, 8):
+        level_total = level_total + lax.ppermute(
+            level_total, "wave", [(dev, dev ^ hop) for dev in range(16)]
+        )
     level_mean = level_total / (NLON * 2.0 * jnp.sum(quad_weights))
     shifted = (tendency - level_mean[None, :, None]).astype(jnp.bfloat16)
     analysed = jnp.einsum(

time: 619 us -> 599 us (0.968)
  blocking collectives: 251 us -> 190 us
  starting transfers between devices: 7.92 us -> 44.6 us
    psum x1 -> x0, blocking collectives: 59.4 us -> none  [per_device(): level_total = lax.psum(partial_sum, 'wave')]
    ppermute x0 -> x4, starting transfers between devices: none -> 36.7 us  [per_device(): lax.ppermute(level_total, 'wave', [(dev, dev ^ hop) for dev in range(16)])]
  transfers between devices with their start and end apart: 1 -> 5, of which waited for: 1 -> 4; matrix products, arithmetic and copies ran while one was open for 2% -> 2% of each run, Pallas kernels for 0% -> 0%
where the time goes in v1:
time: 599 us; the launch traced here: 594 us
  blocking collectives  190 us (32%)
  waiting for transfers between devices  144 us (24%)
  matrix products  82.9 us (14%)
  local copies, waits for them, and re-layouts  81.1 us (14%)
  other arithmetic  50.7 us (8%)
  starting transfers between devices  44.6 us (7%)
    all_to_all x1, blocking collectives, per_device(): lax.all_to_all(folded_part, 'wave', split_axis=0, concat_axis=2, tiled=True)  190 us
    all_to_all x1, waiting for transfers between devices, per_device(): lax.all_to_all(packed, 'wave', split_axis=2, concat_axis=0, tiled=True)  141 us
    ppermute x4, starting transfers between devices, per_device(): lax.ppermute(level_total, 'wave', [(dev, dev ^ hop) for dev in range(16)])  36.7 us
    dot_general x1, matrix products, per_device(): jnp.einsum('mgrv,mrx->gvx', coeff_four, fourier, preferred_element_type=j...  26.1 us
    dot_general x1, matrix products, per_device(): jnp.einsum('uv,gvx->gux', column, grid_temp, precision=lax.Precision.HIGH...  25.1 us
    select_n x1, other arithmetic, per_device(): coeffs = jnp.where(kept_mask, coeffs, jnp.zeros_like(coeffs))  23.7 us
    all_to_all x2, local copies, waits for them, and re-layouts, per_device(): lax.all_to_all(packed, 'wave', split_axis=2, concat_axis=0, tiled=True)  21.4 us
    another operation x1, local copies, waits for them, and re-layouts, per_device(): packed = jnp.stack([north_rows, south_rows], axis=1).astype(jnp.bfloat16)  21 us
  transfers between devices with their start and end apart: 5, of which 4 were waited for; matrix products, arithmetic and copies ran while one was open for 2% of the time, Pallas kernels for 0%

profile of v1, /device:TPU:1, one launch (start us, length us, event | category | flops | bytes accessed | tf_op | source)
XLA Modules:
  0.0 594.4 jit_solution(2933941471523115061)
XLA Ops:
  0.1 7.0 %fusion.14 = f32[32,2,256,192]{2,3,1,0:T(8,128)S(1)} fusion(bf16[32,2,256,256]{3,2,1,0:T(8,128)(2,1)} %param.8, bf16[32,2,256,192]{2,3,1,0:T(8,128)(2,1)} %param.7, pred[32,2,256]{2,1,0:T(4,128)(4,1)S(1)} %add_compare_fusion), kind=kOutput, calls=%fused_computation.34 | convolution fusion | flops 1613758464 | bytes 27279360 | tf_op jit(solution)/shard_map/mpkj,mpkc->mpjc/dot_general | solution.py:34
  7.2 2.7 add_convert_fusion
  9.8 5.2 pad_maximum_fusion
  15.0 21.0 %copy.19 = bf16[32,2,256,192]{3,1,0,2:T(2,128)(2,1)} copy(bf16[32,2,256,192]{2,3,1,0:T(8,128)(2,1)} %pad_maximum_fusion) | data formatting | bytes 12582912 | tf_op jit(solution)/shard_map/stack | solution.py:39
  36.0 7.9 %all-to-all-start = ((bf16[32,2,256,192]{3,1,0,2:T(2,128)(2,1)}), bf16[32,2,256,192]{3,1,0,2:T(2,128)(2,1)}, u32[]{:S(2)}, u32[]{:S(2)}) async-start(bf16[32,2,256,192]{3,1,0,2:T(2,128)(2,1)} %copy.19), calls=%async_computation | async-start | bytes 16777216 | tf_op jit(solution)/shard_map/all_to_all | solution.py:40
  44.1 0.7 gather_fusion.2
  44.8 0.7 gather_fusion.1
  45.6 8.5 %negate_convert_fusion = (bf16[512,1,1024]{2,0,1:T(8,128)(2,1)S(1)}, bf16[512,1,1024]{2,0,1:T(8,128)(2,1)S(1)}) fusion(), kind=kLoop, calls=%fused_computation.47 | loop fusion | flops 8912896 | bytes 2097152 | tf_op jit(solution)/shard_map/convert.7
  54.1 140.9 %all-to-all-done = bf16[32,2,256,192]{3,1,0,2:T(2,128)(2,1)} async-done(((bf16[32,2,256,192]{3,1,0,2:T(2,128)(2,1)}), bf16[32,2,256,192]{3,1,0,2:T(2,128)(2,1)}, u32[]{:S(2)}, u32[]{:S(2)}) %all-to-all-start) | async-done | bytes 6291488 | tf_op jit(solution)/shard_map/all_to_all | solution.py:40
  195.0 13.5 %copy.20 = bf16[32,2,256,192]{3,2,1,0:T(8,128)(2,1)} copy(bf16[32,2,256,192]{3,1,0,2:T(2,128)(2,1)} %all-to-all-done) | data formatting | bytes 12582912 | tf_op jit(solution)/shard_map/all_to_all | solution.py:40
  208.5 7.9 %copy.21 = bf16[16,32,2,16,192]{4,3,2,1,0:T(8,128)(2,1)} copy(bf16[16,32,2,16,192]{4,3,0,2,1:T(8,128)(2,1)} %bitcast.75) | data formatting | bytes 12582912 | tf_op jit(solution)/shard_map/all_to_all | solution.py:40
  216.4 13.8 %reshape.210 = bf16[512,32,2,96]{3,2,1,0:T(2,128)(2,1)} reshape(bf16[16,32,2,16,192]{4,3,2,1,0:T(8,128)(2,1)} %copy.21) | data formatting | bytes 12582912 | tf_op jit(solution)/shard_map/reshape | solution.py:41
  230.1 23.7 %broadcast_select_fusion = bf16[512,32,2,96]{3,2,1,0:T(2,128)(2,1)S(1)} fusion(bf16[512,32,2,96]{3,2,1,0:T(2,128)(2,1)} %reshape.210, pred[512,32]{1,0:T(8,128)(4,1)S(1)} %iota_compare_fusion), kind=kLoop, calls=%fused_computation.4 | loop fusion | flops 3145728 | bytes 12599296 | tf_op jit(solution)/shard_map/jit(_where)/select_n | solution.py:48
  253.9 26.1 %fusion.6 = f32[32,96,1024,1]{2,1,3,0:T(8,128)} fusion(bf16[512,32,2,96]{3,2,1,0:T(2,128)(2,1)S(1)} %broadcast_select_fusion, bf16[512,1,1024]{2,0,1:T(8,128)(2,1)S(1)} %get-tuple-element.11, bf16[512,1,1024]{2,0,1:T(8,128)(2,1)S(1)} %get-tuple-element.12), kind=kOutput, calls=%fused_computation.20 | convolution fusion | flops 6443499520 | bytes 20971520 | tf_op jit(solution)/shard_map/mgrv,mrx->gvx/dot_general | solution.py:51
  279.9 25.1 %multiply_reduce_fusion = (f32[96]{0:T(128)S(1)}, f32[32,96,1024]{2,1,0:T(8,128)}) fusion(f32[32]{0:T(128)S(1)} %gather_fusion.2, f32[96]{0:T(128)S(1)} %get-tuple-element.13, f32[96]{0:T(128)S(1)} %get-tuple-element.14, f32[32,96,1024,1]{2,1,3,0:T(8,128)} %fusion.6, f32[96,96]{1,0:T(8,128)S(1)} %copy-done), kind=kOutput, calls=%fused_computation.19 | convolution fusion | flops 3658481664 | bytes 25203968 | tf_op jit(solution)/shard_map/uv,gvx->gux/dot_general | solution.py:53
  305.1 1.1 collective-permute-done
  306.3 11.5 %collective-permute-start.1 = (f32[96]{0:T(128)S(1)}, f32[96]{0:T(128)S(1)}, u32[]{:S(2)}, u32[]{:S(2)}) collective-permute-start(f32[96]{0:T(128)S(1)} %add.165), channel_id=1, source_target_pairs={{0,2},{1,3},{2,0},{3,1},{4,6},{5,7},{6,4},{7,5},{8,10},{9,11},{10,... | collective-permute-start | bytes 1160 | tf_op jit(solution)/shard_map/ppermute | solution.py:62
  317.8 1.0 collective-permute-done.1
  318.8 22.2 %collective-permute-start.2 = (f32[96]{0:T(128)S(1)}, f32[96]{0:T(128)S(1)}, u32[]{:S(2)}, u32[]{:S(2)}) collective-permute-start(f32[96]{0:T(128)S(1)} %add.166), channel_id=1, source_target_pairs={{0,4},{1,5},{2,6},{3,7},{4,0},{5,1},{6,2},{7,3},{8,12},{9,13},{10,... | collective-permute-start | bytes 1160 | tf_op jit(solution)/shard_map/ppermute | solution.py:62
  341.0 0.9 collective-permute-done.2
  341.9 2.9 collective-permute-start.3
  345.5 0.7 gather_fusion
  346.9 12.5 %multiply_bitcast_fusion = bf16[512,32,2,96]{0,3,1,2:T(8,128)(2,1)S(1)} fusion(f32[32,96,1024]{2,1,0:T(8,128)} %get-tuple-element.10, f32[96]{0:T(128)S(1)} %add_divide_fusion, bf16[512,1,1024]{2,0,1:T(8,128)(2,1)S(1)} %get-tuple-element.11, bf16[512,1,1024]{2,0,1:T(8,128)(2,1)S(1)} %get-tuple-element.12), kind=kOutput, calls=%fused_computation.17 | convolution fusion | flops 6459228160 | bytes 20971904 | tf_op jit(solution)/shard_map/gvx,mrx->mgrv/dot_general | solution.py:67
  359.4 0.7 copy.23
  360.1 2.2 fusion.3
  362.3 1.7 convert_element_type.38
  364.0 2.7 fusion.17
  366.7 3.2 pad_maximum_fusion.1
  369.9 14.2 %copy.24 = bf16[512,2,16,192]{3,2,1,0:T(8,128)(2,1)} copy(bf16[512,2,16,192]{0,3,2,1:T(8,128)(2,1)} %pad_maximum_fusion.1) | data formatting | bytes 12582912 | tf_op jit(solution)/shard_map/stack | solution.py:76
  384.1 190.0 %all_to_all.33 = bf16[512,2,16,192]{3,2,1,0:T(8,128)(2,1)} all-to-all(bf16[512,2,16,192]{3,2,1,0:T(8,128)(2,1)} %copy.24), channel_id=1, replica_groups=mesh['member'=2,'wave'=16] {'wave'}, dimensions={0} | all-to-all | bytes 12582912 | tf_op jit(solution)/shard_map/all_to_all | solution.py:79
  574.1 7.9 %copy.25 = bf16[32,2,16,16,192]{4,3,2,1,0:T(8,128)(2,1)} copy(bf16[32,2,16,16,192]{4,3,1,0,2:T(8,128)(2,1)} %bitcast.76) | data formatting | bytes 12582912 | tf_op jit(solution)/shard_map/all_to_all | solution.py:79
  581.9 12.3 %fusion.2 = bf16[32,2,256,192]{2,3,1,0:T(8,128)(2,1)} fusion(pred[32,2,256]{2,1,0:T(4,128)(4,1)S(1)} %add_compare_fusion, bf16[32,2,256,192]{2,3,1,0:T(8,128)(2,1)} %param.7, bf16[32,2,256,192]{3,2,1,0:T(8,128)(2,1)} %bitcast.77, bf16[32,2,256,256]{3,2,1,0:T(8,128)(2,1)} %param.8), kind=kOutput, calls=%fused_computation.8 | convolution fusion | flops 1626341376 | bytes 27279360 | tf_op jit(solution)/shard_map/mpkj,mpjc->mpkc/dot_general | solution.py:80
  (31 shorter events, 1.1 us)
Async XLA Ops:
  0.0 279.9 %copy-start = (f32[96,96]{1,0:T(8,128)S(1)}, f32[96,96]{1,0:T(8,128)}, u32[]{:S(2)}) copy-start(f32[96,96]{1,0:T(8,128)} %param.10) | copy-start | bytes 110596
  36.0 8.0 %copy-start.2 = (f32[256]{0:T(256)S(1)}, f32[256]{0:T(256)}, u32[]{:S(2)}) copy-start(f32[256]{0:T(256)} %param.9) | copy-start | bytes 3076
  36.0 8.8 %copy-start.3 = (s32[256]{0:T(256)S(1)}, s32[256]{0:T(256)}, u32[]{:S(2)}) copy-start(s32[256]{0:T(256)} %param.13) | copy-start | bytes 3076
  36.0 9.5 %copy-start.4 = (f32[96]{0:T(128)S(1)}, f32[96]{0:T(128)}, u32[]{:S(2)}) copy-start(f32[96]{0:T(128)} %param.12) | copy-start | bytes 1156
  36.0 9.5 %copy-start.5 = (f32[96]{0:T(128)S(1)}, f32[96]{0:T(128)}, u32[]{:S(2)}) copy-start(f32[96]{0:T(128)} %param.11) | copy-start | bytes 1156
  36.0 158.9 %all-to-all-start = ((bf16[32,2,256,192]{3,1,0,2:T(2,128)(2,1)}), bf16[32,2,256,192]{3,1,0,2:T(2,128)(2,1)}, u32[]{:S(2)}, u32[]{:S(2)}) async-start(bf16[32,2,256,192]{3,1,0,2:T(2,128)(2,1)} %copy.19), calls=%async_computation | async-start | bytes 16777216 | tf_op jit(solution)/shard_map/all_to_all | solution.py:40
  305.1 1.2 collective-permute-start
  306.3 12.5 %collective-permute-start.1 = (f32[96]{0:T(128)S(1)}, f32[96]{0:T(128)S(1)}, u32[]{:S(2)}, u32[]{:S(2)}) collective-permute-start(f32[96]{0:T(128)S(1)} %add.165), channel_id=1, source_target_pairs={{0,2},{1,3},{2,0},{3,1},{4,6},{5,7},{6,4},{7,5},{8,10},{9,11},{10,... | collective-permute-start | bytes 1160 | tf_op jit(solution)/shard_map/ppermute | solution.py:62
  318.8 23.1 %collective-permute-start.2 = (f32[96]{0:T(128)S(1)}, f32[96]{0:T(128)S(1)}, u32[]{:S(2)}, u32[]{:S(2)}) collective-permute-start(f32[96]{0:T(128)S(1)} %add.166), channel_id=1, source_target_pairs={{0,4},{1,5},{2,6},{3,7},{4,0},{5,1},{6,2},{7,3},{8,12},{9,13},{10,... | collective-permute-start | bytes 1160 | tf_op jit(solution)/shard_map/ppermute | solution.py:62
  341.9 4.9 collective-permute-start.3
  581.9 12.3 %copy-start.1 = (f32[96,96]{1,0:T(8,128)S(1)}, f32[96,96]{1,0:T(8,128)}, u32[]{:S(2)}) copy-start(f32[96,96]{1,0:T(8,128)} %param.10) | copy-start | bytes 110596
